TPU v7x, 32 devices: a whole 2x2x4 slice. The times are simulated.
32 devices in a mesh: rep: 2 (over x), ea: 16 (over z, y, core).
Axes of the slice: x: 2, y: 2, z: 4, core: 2. Of those that a mesh axis runs over, the one named last changes fastest.
Arguments:
- hidden_in: bfloat16 [512, 4, 4096], P('ea', 'rep'), parts along dimension 1, may hold values from -3 to 3
- queries: bfloat16 [32, 512, 512], P(('rep', 'ea')), parts along dimension 0, may hold values from -112 to 112, as said below
- cache_keys: bfloat16 [32, 512, 128], P(('rep', 'ea')), parts along dimension 0, may hold values from -4 to 4
- cache_values: bfloat16 [32, 512, 128], P(('rep', 'ea')), parts along dimension 0, may hold values from -24 to 24
- new_keys: bfloat16 [32, 512, 128], P(('rep', 'ea')), parts along dimension 0, may hold values from -6 to 6
- new_values: bfloat16 [32, 512, 128], P(('rep', 'ea')), parts along dimension 0, may hold values from -24 to 24
- cache_len: int32 [4], P('rep'), parts along dimension 0, may hold values from 128 to 512, as said below
- out_proj: bfloat16 [4096, 4096], P(None, 'ea'), may hold values from -0.25 to 0.25
- norm_gain: float32 [4096], replicated, may hold values from 0.25 to 1.75
- router: bfloat16 [4096, 16], replicated, may hold values from -0.09375 to 0.09375
- expert_ids: int32 [512, 4, 2], P('ea', 'rep'), parts along dimension 1, may hold values from 0 to 15, all different within a row; in each aligned block of 64 rows (0 to 63, 64 to 127, ..., all dimensions but the last counted through in order) at most 9 rows name the same one
- gate_proj: bfloat16 [4096, 51200], P(None, 'ea'), may hold values from -0.09375 to 0.09375
- up_proj: bfloat16 [4096, 51200], P(None, 'ea'), may hold values from -0.09375 to 0.09375
- down_proj: bfloat16 [51200, 4096], P('ea'), may hold values from -0.109375 to 0.109375
Outputs:
- layer_out: bfloat16 [512, 4, 4096], P('ea', 'rep'), parts along dimension 1
There are 2 independent parts, one for each index of `rep`. A program takes and returns all parts, laid end to end along the dimension named above; an argument that names none is the same for every part. Nothing has to cross between parts.
Inputs may be any that keep to these rules, and one draw needn't show every extreme that they name: `queries`: each entry of the hidden draw may reach the stated range. `cache_len`: some sequence has exactly 512 filled slots. `expert_ids`: the two experts of a row differ. Rows are taken in order of the first two dimensions; in each aligned block of 64 rows (the rows of one device) no expert is named by more than 9 rows, and in some block one expert is named by exactly 9 rows; every expert is named somewhere.
All inputs are finite; a program needn't handle non-finite values.
Results may differ from a plain program's by a relative error of at most 0.0068.
Values may be sent and summed in bfloat16 or wider, within the bound.
A program may use at most 192 MiB of HBM per device.

v0:
```python
import math

import jax
import jax.numpy as jnp
from jax import lax
from jax.sharding import PartitionSpec as P

HQ = 32
KVH = 8
HD = 128
EXPERTS = 16
TOPK = 2
CAP = 9


def expert_terms(received, gate_proj, up_proj, down_proj):
    src_count, slot_count, model_width = received.shape
    flat_rows = received.reshape(src_count * slot_count, model_width)
    gate_val = jnp.dot(flat_rows, gate_proj, preferred_element_type=jnp.float32)
    up_val = jnp.dot(flat_rows, up_proj, preferred_element_type=jnp.float32)
    inner_act = (jax.nn.silu(gate_val) * up_val).astype(jnp.bfloat16)
    shard_term = jnp.dot(inner_act, down_proj, preferred_element_type=jnp.float32).astype(
        jnp.bfloat16
    )
    return shard_term.reshape(src_count, slot_count, model_width)


def expert_half(received, gate_proj, up_proj, down_proj):
    shard_term = expert_terms(received, gate_proj, up_proj, down_proj)
    return lax.all_to_all(shard_term, "ea", split_axis=0, concat_axis=0, tiled=True)


def route_rows(normed, route_ids, first_gate, gate_proj, up_proj, down_proj):
    row_count, model_width = normed.shape
    dev_count = lax.axis_size("ea")
    shard_count = dev_count // EXPERTS
    flat_ids = route_ids.reshape(-1)
    pair_count = flat_ids.shape[0]
    expert_cols = jnp.arange(EXPERTS, dtype=jnp.int32)
    one_hot = (flat_ids[:, None] == expert_cols[None, :]).astype(jnp.float32)
    pair_order = jnp.arange(pair_count, dtype=jnp.int32)
    earlier = (pair_order[:, None] > pair_order[None, :]).astype(jnp.float32)
    before = jnp.dot(earlier, one_hot, precision=lax.Precision.HIGHEST)
    slot_pos = jnp.sum(before * one_hot, axis=1).astype(jnp.int32)
    target = (flat_ids * CAP + slot_pos).reshape(row_count, TOPK)
    slot_ids = jnp.arange(EXPERTS * CAP, dtype=jnp.int32)
    select = (
        (target[None, :, 0] == slot_ids[:, None]) | (target[None, :, 1] == slot_ids[:, None])
    ).astype(jnp.bfloat16)
    packed = jnp.dot(select, normed, preferred_element_type=jnp.float32).astype(jnp.bfloat16)
    packed = jnp.broadcast_to(
        packed.reshape(EXPERTS, 1, CAP, model_width), (EXPERTS, shard_count, CAP, model_width)
    )
    packed = packed.reshape(dev_count, CAP, model_width)
    first_slots = (CAP + 1) // 2
    bounds = [(0, first_slots), (first_slots, CAP)]
    pieces = []
    for lower, upper in bounds:
        part_block = packed[:, lower:upper]
        pieces.append(
            (lambda received: expert_half(received, gate_proj, up_proj, down_proj))(
                lax.all_to_all(part_block, "ea", split_axis=0, concat_axis=0, tiled=True)
            )
        )
    returned = jnp.concatenate(pieces, axis=1)
    expert_out = jnp.sum(
        returned.reshape(EXPERTS, shard_count, CAP, model_width).astype(jnp.float32), axis=1
    )
    expert_out = expert_out.reshape(EXPERTS * CAP, model_width)
    picked = jnp.take(expert_out, target, axis=0)
    return first_gate * picked[:, 0] + (1.0 - first_gate) * picked[:, 1]


def body(
    hidden_in,
    queries,
    cache_keys,
    cache_values,
    new_keys,
    new_values,
    cache_len,
    out_proj,
    norm_gain,
    router,
    expert_ids,
    gate_proj,
    up_proj,
    down_proj,
):
    dev_count = lax.axis_size("ea")
    dev_index = lax.axis_index("ea")
    new_rows = queries.shape[1]
    group_q = HQ // KVH
    seq_count = dev_count // KVH
    piece_rows = new_rows // dev_count
    cache_rows = cache_keys.shape[1]
    col_width = out_proj.shape[1]
    model_width = hidden_in.shape[2]
    score_scale = 1.0 / math.sqrt(HD)
    visible = lax.dynamic_index_in_dim(cache_len, dev_index // KVH, keepdims=False)
    position = (
        jnp.arange(new_rows, dtype=jnp.int32).reshape(dev_count, piece_rows).T.reshape(new_rows)
    )
    query_rows = (
        queries[0]
        .reshape(dev_count, piece_rows, group_q, HD)
        .transpose(1, 0, 2, 3)
        .reshape(new_rows, group_q, HD)
    )
    all_keys = jnp.concatenate([cache_keys[0], new_keys[0]], axis=0)
    all_values = jnp.concatenate([cache_values[0], new_values[0]], axis=0)
    key_pos = jnp.arange(cache_rows + new_rows, dtype=jnp.int32)
    allowed = jnp.where(
        key_pos[None, :] < cache_rows,
        key_pos[None, :] < visible,
        key_pos[None, :] - cache_rows <= position[:, None],
    )
    scores = (
        jnp.einsum("qhd,kd->hqk", query_rows, all_keys, preferred_element_type=jnp.float32)
        * score_scale
    )
    scores = jnp.where(allowed[None], scores, jnp.float32(-1e30))
    top_score = jnp.max(scores, axis=2, keepdims=True)
    exp_scores = jnp.exp(scores - top_score)
    attn_probs = (exp_scores / jnp.sum(exp_scores, axis=2, keepdims=True)).astype(jnp.bfloat16)
    attended = jnp.einsum("hqk,kd->qhd", attn_probs, all_values, preferred_element_type=jnp.float32)
    attended = attended.astype(jnp.bfloat16).reshape(new_rows, group_q * HD)
    local_rows = out_proj.reshape(KVH, group_q * HD, col_width).transpose(1, 0, 2)
    outgoing = jnp.broadcast_to(local_rows[:, None], (group_q * HD, seq_count, KVH, col_width))
    outgoing = outgoing.reshape(group_q * HD, dev_count, col_width)
    group_proj = lax.all_to_all(outgoing, "ea", split_axis=1, concat_axis=1, tiled=True).reshape(
        group_q * HD, model_width
    )
    head_part = jnp.dot(attended, group_proj, preferred_element_type=jnp.float32).astype(
        jnp.bfloat16
    )
    arrived = lax.all_to_all(
        head_part.reshape(piece_rows, dev_count, model_width),
        "ea",
        split_axis=1,
        concat_axis=1,
        tiled=True,
    )
    head_sum = jnp.sum(
        arrived.reshape(piece_rows, seq_count, KVH, model_width).astype(jnp.float32), axis=2
    )
    residual = hidden_in.astype(jnp.float32) + head_sum
    flat_res = residual.reshape(piece_rows * seq_count, model_width)
    mean_sq = jnp.mean(flat_res * flat_res, axis=1, keepdims=True)
    normed = (flat_res * lax.rsqrt(mean_sq + 1e-05) * norm_gain[None, :]).astype(jnp.bfloat16)
    logits = jnp.dot(normed, router, preferred_element_type=jnp.float32)
    route_ids = expert_ids.reshape(piece_rows * seq_count, TOPK)
    chosen = jnp.take_along_axis(logits, route_ids, axis=1)
    first_gate = jax.nn.sigmoid(chosen[:, 0:1] - chosen[:, 1:2])
    expert_mix = route_rows(normed, route_ids, first_gate, gate_proj, up_proj, down_proj)
    result_rows = (flat_res + expert_mix).astype(jnp.bfloat16)
    return result_rows.reshape(piece_rows, seq_count, model_width)


def solution(mesh):
    placed = (
        P("ea", "rep", None),
        P(("rep", "ea"), None, None),
        P(("rep", "ea"), None, None),
        P(("rep", "ea"), None, None),
        P(("rep", "ea"), None, None),
        P(("rep", "ea"), None, None),
        P("rep"),
        P(None, "ea"),
        P(),
        P(),
        P("ea", "rep", None),
        P(None, "ea"),
        P(None, "ea"),
        P("ea", None),
    )
    return jax.shard_map(
        body, mesh=mesh, in_specs=placed, out_specs=P("ea", "rep", None), check_vma=False
    )
```

profile of v0, /device:TPU:9, one launch (start us, length us, event | category | flops | bytes accessed | tf_op | source)
XLA Modules:
  0.0 377.9 jit_solution(7434829781449206747)
XLA Ops:
  0.0 4.0 %broadcast_in_dim.65 = bf16[512,2,8,256]{3,0,2,1:T(8,128)(2,1)} broadcast(bf16[512,8,256]{2,0,1:T(8,128)(2,1)} %bitcast.84), dimensions={0,2,3} | broadcast | bytes 6291456 | tf_op jit(solution)/shard_map/broadcast_in_dim | solution.py:129
  4.1 6.8 %all-to-all-start = ((bf16[512,16,256]{2,0,1:T(8,128)(2,1)}), bf16[512,16,256]{2,0,1:T(8,128)(2,1)}, u32[]{:S(2)}, u32[]{:S(2)}) async-start(bf16[512,16,256]{2,0,1:T(8,128)(2,1)} %bitcast.81), calls=%async_computation | async-start | bytes 8388608 | tf_op jit(solution)/shard_map/all_to_all | solution.py:131
  13.9 6.3 %fusion.50 = (f32[4,512]{1,0:T(4,128)S(1)}, f32[4,512,1024]{1,2,0:T(8,128)}) fusion(pred[512,1024]{0,1:T(8,128)(4,1)S(1)} %compare_select_fusion, bf16[512,4,128]{2,0,1:T(8,128)(2,1)S(1)} %bitcast.86, bf16[512,128]{1,0:T(8,128)(2,1)S(1)} %bitcast.89, bf16[512,128]{1,0:T(8,128)(2,1)S(1)} %bitcast.90), kind=kOutput, calls=%fused_computation.90 | convolution fusion | flops 545784832 | bytes 9707520 | tf_op jit(solution)/shard_map/sub | solution.py:124
  20.3 4.1 %fusion.8 = bf16[128,4,512]{2,0,1:T(8,128)(2,1)S(1)} fusion(f32[4,512,1024]{1,2,0:T(8,128)} %get-tuple-element.18, f32[4,512]{1,0:T(4,128)S(1)} %get-tuple-element.17, bf16[512,128]{0,1:T(8,128)(2,1)S(1)} %bitcast.88, bf16[512,128]{0,1:T(8,128)(2,1)S(1)} %bitcast.87), kind=kOutput, calls=%fused_computation.23 | convolution fusion | flops 541851648 | bytes 9183232 | tf_op jit(solution)/shard_map/hqk,kd->qhd/dot_general | solution.py:126
  24.4 76.7 %all-to-all-done = bf16[512,16,256]{2,0,1:T(8,128)(2,1)} async-done(((bf16[512,16,256]{2,0,1:T(8,128)(2,1)}), bf16[512,16,256]{2,0,1:T(8,128)(2,1)}, u32[]{:S(2)}, u32[]{:S(2)}) %all-to-all-start) | async-done | bytes 4194336 | tf_op jit(solution)/shard_map/all_to_all | solution.py:131
  101.1 6.4 %copy.118 = bf16[512,16,256]{0,2,1:T(8,128)(2,1)} copy(bf16[512,16,256]{2,0,1:T(8,128)(2,1)} %all-to-all-done) | data formatting | bytes 8388608 | tf_op jit(solution)/shard_map/all_to_all | solution.py:131
  107.6 4.6 %convolution_convert_fusion = bf16[512,4096]{1,0:T(8,128)(2,1)S(1)} fusion(bf16[512,512]{0,1:T(8,128)(2,1)S(1)} %bitcast.91, bf16[512,4096]{0,1:T(8,128)(2,1)} %bitcast.82), kind=kOutput, calls=%fused_computation.8 | convolution fusion | flops 2149580800 | bytes 8912896 | tf_op jit(solution)/shard_map/dot_general | solution.py:134
  112.2 4.3 %copy.119 = bf16[32,16,4096]{2,0,1:T(8,128)(2,1)} copy(bf16[32,16,4096]{2,1,0:T(8,128)(2,1)S(1)} %bitcast.83) | data formatting | bytes 8388608 | tf_op jit(solution)/shard_map/reshape | solution.py:138
  116.4 7.2 %all-to-all-start.1 = ((bf16[32,16,4096]{2,0,1:T(8,128)(2,1)}), bf16[32,16,4096]{2,0,1:T(8,128)(2,1)}, u32[]{:S(2)}, u32[]{:S(2)}) async-start(bf16[32,16,4096]{2,0,1:T(8,128)(2,1)} %copy.119), calls=%async_computation.1 | async-start | bytes 8388608 | tf_op jit(solution)/shard_map/all_to_all | solution.py:137
  125.1 88.8 %all-to-all-done.1 = bf16[32,16,4096]{2,0,1:T(8,128)(2,1)} async-done(((bf16[32,16,4096]{2,0,1:T(8,128)(2,1)}), bf16[32,16,4096]{2,0,1:T(8,128)(2,1)}, u32[]{:S(2)}, u32[]{:S(2)}) %all-to-all-start.1) | async-done | bytes 4194336 | tf_op jit(solution)/shard_map/all_to_all | solution.py:137
  213.9 3.0 convert_reduce_fusion
  217.7 1.8 copy.121
  219.5 1.9 reshape.277
  221.6 1.5 convolution_convert_fusion.1
  223.2 2.6 reshape_reshape.4
  225.8 2.7 slice.37
  228.5 7.1 %all-to-all-start.4 = ((bf16[16,4,4096]{2,1,0:T(4,128)(2,1)}), bf16[16,4,4096]{2,1,0:T(4,128)(2,1)S(1)}, u32[]{:S(2)}, u32[]{:S(2)}) async-start(bf16[16,4,4096]{2,1,0:T(4,128)(2,1)} %slice.37), calls=%async_computation.4 | async-start | bytes 1048576 | tf_op jit(solution)/shard_map/all_to_all | solution.py:62
  235.6 2.3 slice.36
  237.9 11.8 %all-to-all-done.4 = bf16[16,4,4096]{2,1,0:T(4,128)(2,1)S(1)} async-done(((bf16[16,4,4096]{2,1,0:T(4,128)(2,1)}), bf16[16,4,4096]{2,1,0:T(4,128)(2,1)S(1)}, u32[]{:S(2)}, u32[]{:S(2)}) %all-to-all-start.4) | async-done | bytes 524320 | tf_op jit(solution)/shard_map/all_to_all | solution.py:62
  249.7 4.5 %all-to-all-start.2 = ((bf16[16,5,4096]{2,1,0:T(8,128)(2,1)}), bf16[16,5,4096]{2,1,0:T(8,128)(2,1)}, u32[]{:S(2)}, u32[]{:S(2)}) async-start(bf16[16,5,4096]{2,1,0:T(8,128)(2,1)} %slice.36), calls=%async_computation.2 | async-start | bytes 2097152 | tf_op jit(solution)/shard_map/all_to_all | solution.py:62
  254.4 11.9 %fusion.52 = f32[64,3200]{1,0:T(8,128)} fusion(bf16[64,4096]{1,0:T(8,128)(2,1)S(1)} %reshape.281, bf16[4096,3200]{1,0:T(8,128)(2,1)} %param.25), kind=kOutput, calls=%fused_computation.92 | convolution fusion | flops 1677721600 | bytes 27557888 | tf_op jit(solution)/shard_map/dot_general | solution.py:19
  266.2 19.9 %convolution_convert_fusion.3 = bf16[64,4096]{1,0:T(8,128)(2,1)S(1)} fusion(bf16[3200,4096]{1,0:T(8,128)(2,1)} %param.27, bf16[64,4096]{1,0:T(8,128)(2,1)S(1)} %reshape.281, bf16[4096,3200]{1,0:T(8,128)(2,1)} %param.26, f32[64,3200]{1,0:T(8,128)} %fusion.52), kind=kOutput, calls=%fused_computation.15 | convolution fusion | flops 3356934144 | bytes 54296576 | tf_op jit(solution)/shard_map/dot_general | solution.py:22
  287.1 6.1 %all-to-all-start.5 = ((bf16[16,4,4096]{2,1,0:T(4,128)(2,1)}), bf16[16,4,4096]{2,1,0:T(4,128)(2,1)}, u32[]{:S(2)}, u32[]{:S(2)}) async-start(bf16[16,4,4096]{2,1,0:T(4,128)(2,1)} %reshape.282), calls=%async_computation.5 | async-start | bytes 1048576 | tf_op jit(solution)/shard_map/all_to_all | solution.py:30
  294.7 11.9 %fusion.51 = f32[80,3200]{1,0:T(8,128)} fusion(bf16[80,4096]{1,0:T(8,128)(2,1)S(1)} %reshape.279, bf16[4096,3200]{1,0:T(8,128)(2,1)} %param.25), kind=kOutput, calls=%fused_computation.91 | convolution fusion | flops 2097152000 | bytes 27893760 | tf_op jit(solution)/shard_map/dot_general | solution.py:19
  306.6 20.0 %convolution_convert_fusion.2 = bf16[80,4096]{1,0:T(8,128)(2,1)S(1)} fusion(bf16[3200,4096]{1,0:T(8,128)(2,1)} %param.27, bf16[80,4096]{1,0:T(8,128)(2,1)S(1)} %reshape.279, bf16[4096,3200]{1,0:T(8,128)(2,1)} %param.26, f32[80,3200]{1,0:T(8,128)} %fusion.51), kind=kOutput, calls=%fused_computation.13 | convolution fusion | flops 4196167680 | bytes 54763520 | tf_op jit(solution)/shard_map/dot_general | solution.py:22
  327.9 6.0 %all-to-all-start.3 = ((bf16[16,5,4096]{2,1,0:T(8,128)(2,1)}), bf16[16,5,4096]{2,1,0:T(8,128)(2,1)}, u32[]{:S(2)}, u32[]{:S(2)}) async-start(bf16[16,5,4096]{2,1,0:T(8,128)(2,1)} %reshape.280), calls=%async_computation.3 | async-start | bytes 2097152 | tf_op jit(solution)/shard_map/all_to_all | solution.py:30
  339.6 19.2 %all-to-all-done.3 = bf16[16,5,4096]{2,1,0:T(8,128)(2,1)} async-done(((bf16[16,5,4096]{2,1,0:T(8,128)(2,1)}), bf16[16,5,4096]{2,1,0:T(8,128)(2,1)}, u32[]{:S(2)}, u32[]{:S(2)}) %all-to-all-start.3) | async-done | bytes 655392 | tf_op jit(solution)/shard_map/all_to_all | solution.py:30
  358.8 4.1 %maximum_convert_fusion = f32[16,1,9,4096]{3,2,0,1:T(8,128)} fusion(bf16[16,1,4,4096]{3,2,0,1:T(4,128)(2,1)} %bitcast.21, bf16[16,1,5,4096]{3,2,0,1:T(8,128)(2,1)} %bitcast.20), kind=kLoop, calls=%fused_computation.20 | loop fusion | flops 2359296 | bytes 3538944 | tf_op jit(solution)/shard_map/convert_element_type | solution.py:67
  362.9 2.4 reshape.284
  365.3 2.5 gather_fusion
  367.9 2.5 reshape.286
  373.5 1.8 squeeze.28
  (79 shorter events, 20.6 us)
Async XLA Ops:
  0.0 335.5 %copy-start = (bf16[4096,16]{0,1:T(8,128)(2,1)S(1)}, bf16[4096,16]{0,1:T(8,128)(2,1)}, u32[]{:S(2)}) copy-start(bf16[4096,16]{0,1:T(8,128)(2,1)} %param.23) | copy-start | bytes 393220
  4.0 6.9 %copy-start.2 = (bf16[1,512,512]{2,1,0:T(8,128)(2,1)S(1)}, bf16[1,512,512]{2,1,0:T(8,128)(2,1)}, u32[]{:S(2)}) copy-start(bf16[1,512,512]{2,1,0:T(8,128)(2,1)} %param.15) | copy-start | bytes 1572868
  4.0 7.4 %copy-start.4 = (bf16[1,512,128]{2,1,0:T(8,128)(2,1)S(1)}, bf16[1,512,128]{2,1,0:T(8,128)(2,1)}, u32[]{:S(2)}) copy-start(bf16[1,512,128]{2,1,0:T(8,128)(2,1)} %param.17) | copy-start | bytes 393220
  4.0 7.5 %copy-start.5 = (bf16[1,512,128]{2,1,0:T(8,128)(2,1)S(1)}, bf16[1,512,128]{2,1,0:T(8,128)(2,1)}, u32[]{:S(2)}) copy-start(bf16[1,512,128]{2,1,0:T(8,128)(2,1)} %param.19) | copy-start | bytes 393220
  4.0 7.6 %copy-start.11 = (s32[2]{0:T(128)S(1)}, s32[2]{0:T(128)}, u32[]{:S(2)}) copy-start(s32[2]{0:T(128)} %param.20) | copy-start | bytes 28
  4.1 9.9 %copy-start.9 = (bf16[1,512,128]{2,1,0:T(8,128)(2,1)S(1)}, bf16[1,512,128]{2,1,0:T(8,128)(2,1)}, u32[]{:S(2)}) copy-start(bf16[1,512,128]{2,1,0:T(8,128)(2,1)} %param.18) | copy-start | bytes 393220
  4.1 9.9 %copy-start.10 = (bf16[1,512,128]{2,1,0:T(8,128)(2,1)S(1)}, bf16[1,512,128]{2,1,0:T(8,128)(2,1)}, u32[]{:S(2)}) copy-start(bf16[1,512,128]{2,1,0:T(8,128)(2,1)} %param.16) | copy-start | bytes 393220
  4.1 97.1 %all-to-all-start = ((bf16[512,16,256]{2,0,1:T(8,128)(2,1)}), bf16[512,16,256]{2,0,1:T(8,128)(2,1)}, u32[]{:S(2)}, u32[]{:S(2)}) async-start(bf16[512,16,256]{2,0,1:T(8,128)(2,1)} %bitcast.81), calls=%async_computation | async-start | bytes 8388608 | tf_op jit(solution)/shard_map/all_to_all | solution.py:131
  116.4 7.2 %copy-start.7 = (s32[32,2,2]{0,2,1:T(2,128)S(1)}, s32[32,2,2]{0,2,1:T(2,128)}, u32[]{:S(2)}) copy-start(s32[32,2,2]{0,2,1:T(2,128)} %param.24) | copy-start | bytes 1540
  116.4 97.5 %all-to-all-start.1 = ((bf16[32,16,4096]{2,0,1:T(8,128)(2,1)}), bf16[32,16,4096]{2,0,1:T(8,128)(2,1)}, u32[]{:S(2)}, u32[]{:S(2)}) async-start(bf16[32,16,4096]{2,0,1:T(8,128)(2,1)} %copy.119), calls=%async_computation.1 | async-start | bytes 8388608 | tf_op jit(solution)/shard_map/all_to_all | solution.py:137
  123.6 93.3 %copy-start.1 = (bf16[32,2,4096]{2,1,0:T(2,128)(2,1)S(1)}, bf16[32,2,4096]{2,1,0:T(2,128)(2,1)}, u32[]{:S(2)}) copy-start(bf16[32,2,4096]{2,1,0:T(2,128)(2,1)} %param.14) | copy-start | bytes 1572868
  123.8 95.6 %copy-start.3 = (s32[32,2,2]{1,0,2:T(8,128)}, s32[32,2,2]{1,0,2:T(8,128)S(1)}, u32[]{:S(2)}) copy-start(s32[32,2,2]{1,0,2:T(8,128)S(1)} %copy.120) | copy-start | bytes 1540
  216.9 4.7 %copy-start.6 = (f32[4096]{0:T(1024)S(1)}, f32[4096]{0:T(1024)}, u32[]{:S(2)}) copy-start(f32[4096]{0:T(1024)} %param.22) | copy-start | bytes 49156
  228.5 21.2 %all-to-all-start.4 = ((bf16[16,4,4096]{2,1,0:T(4,128)(2,1)}), bf16[16,4,4096]{2,1,0:T(4,128)(2,1)S(1)}, u32[]{:S(2)}, u32[]{:S(2)}) async-start(bf16[16,4,4096]{2,1,0:T(4,128)(2,1)} %slice.37), calls=%async_computation.4 | async-start | bytes 1048576 | tf_op jit(solution)/shard_map/all_to_all | solution.py:62
  249.7 37.4 %all-to-all-start.2 = ((bf16[16,5,4096]{2,1,0:T(8,128)(2,1)}), bf16[16,5,4096]{2,1,0:T(8,128)(2,1)}, u32[]{:S(2)}, u32[]{:S(2)}) async-start(bf16[16,5,4096]{2,1,0:T(8,128)(2,1)} %slice.36), calls=%async_computation.2 | async-start | bytes 2097152 | tf_op jit(solution)/shard_map/all_to_all | solution.py:62
  287.1 40.7 %all-to-all-start.5 = ((bf16[16,4,4096]{2,1,0:T(4,128)(2,1)}), bf16[16,4,4096]{2,1,0:T(4,128)(2,1)}, u32[]{:S(2)}, u32[]{:S(2)}) async-start(bf16[16,4,4096]{2,1,0:T(4,128)(2,1)} %reshape.282), calls=%async_computation.5 | async-start | bytes 1048576 | tf_op jit(solution)/shard_map/all_to_all | solution.py:30
  327.9 31.0 %all-to-all-start.3 = ((bf16[16,5,4096]{2,1,0:T(8,128)(2,1)}), bf16[16,5,4096]{2,1,0:T(8,128)(2,1)}, u32[]{:S(2)}, u32[]{:S(2)}) async-start(bf16[16,5,4096]{2,1,0:T(8,128)(2,1)} %reshape.280), calls=%async_computation.3 | async-start | bytes 2097152 | tf_op jit(solution)/shard_map/all_to_all | solution.py:30
  367.9 2.5 copy-start.8
where the time goes:
time: 379 us; the launch traced here: 378 us
  waiting for transfers between devices  197 us (52%)
  matrix products  81.4 us (21%)
  local copies, waits for them, and re-layouts  48.6 us (13%)
  starting transfers between devices  37.6 us (10%)
  other arithmetic  13.3 us (4%)
    all_to_all x1, waiting for transfers between devices, body(): lax.all_to_all(head_part.reshape(piece_rows, dev_count, model_width), 'ea...  88.8 us
    all_to_all x1, waiting for transfers between devices, body(): lax.all_to_all(outgoing, 'ea', split_axis=1, concat_axis=1, tiled=True)  76.7 us
    dot_general x2, matrix products, expert_terms(): jnp.dot(inner_act, down_proj, preferred_element_type=jnp.float32)  39.9 us
    dot_general x2, matrix products, expert_terms(): gate_val = jnp.dot(flat_rows, gate_proj, preferred_element_type=jnp.float32)  23.8 us
    all_to_all x2, waiting for transfers between devices, expert_half(): lax.all_to_all(shard_term, 'ea', split_axis=0, concat_axis=0, tiled=True)  19.2 us
    all_to_all x2, starting transfers between devices, expert_half(): lax.all_to_all(shard_term, 'ea', split_axis=0, concat_axis=0, tiled=True)  12.1 us
    all_to_all x2, waiting for transfers between devices, route_rows(): lax.all_to_all(part_block, 'ea', split_axis=0, concat_axis=0, tiled=True)  11.8 us
    all_to_all x2, starting transfers between devices, route_rows(): lax.all_to_all(part_block, 'ea', split_axis=0, concat_axis=0, tiled=True)  11.6 us
  transfers between devices with their start and end apart: 6, of which 4 were waited for; matrix products, arithmetic and copies ran while one was open for 24% of the time, Pallas kernels for 0%

commit v1 on v0

--- a/solution.py
+++ b/solution.py
@@ -1,8 +1,11 @@
+import functools
 import math
 
 import jax
 import jax.numpy as jnp
 from jax import lax
+from jax.experimental import pallas as pl
+from jax.experimental.pallas import tpu as pltpu
 from jax.sharding import PartitionSpec as P
 
 HQ = 32
@@ -71,7 +74,7 @@
     return first_gate * picked[:, 0] + (1.0 - first_gate) * picked[:, 1]
 
 
-def body(
+def wide_body(
     hidden_in,
     queries,
     cache_keys,
@@ -157,6 +160,464 @@
     return result_rows.reshape(piece_rows, seq_count, model_width)
 
 
+NZ = 4
+NDEV = 16
+MAIN = 8
+SLOTS = EXPERTS * CAP
+F32 = jnp.float32
+BF16 = jnp.bfloat16
+
+
+def attend_kernel(len_ref, q_ref, ck_ref, cv_ref, nk_ref, nv_ref, o_ref, *, seq_devs):
+    visible = len_ref[lax.axis_index("ea") // seq_devs]
+    contract = (((1,), (1,)), ((), ()))
+    q = q_ref[...]
+    rows, cached, fresh = q.shape[0], ck_ref.shape[0], nk_ref.shape[0]
+    scale = 1.0 / math.sqrt(HD)
+    old = lax.dot_general(q, ck_ref[...], contract, preferred_element_type=F32) * scale
+    new = lax.dot_general(q, nk_ref[...], contract, preferred_element_type=F32) * scale
+    old_pos = lax.broadcasted_iota(jnp.int32, (rows, cached), 1)
+    row_pos = lax.broadcasted_iota(jnp.int32, (rows, fresh), 0)
+    new_pos = lax.broadcasted_iota(jnp.int32, (rows, fresh), 1)
+    old = jnp.where(old_pos < visible, old, -1e30)
+    new = jnp.where(new_pos <= row_pos, new, -1e30)
+    top = jnp.maximum(
+        jnp.max(old, axis=1, keepdims=True), jnp.max(new, axis=1, keepdims=True)
+    )
+    old = jnp.exp(old - top)
+    new = jnp.exp(new - top)
+    total = jnp.sum(old, axis=1, keepdims=True) + jnp.sum(new, axis=1, keepdims=True)
+    mixed = jnp.dot(old.astype(BF16), cv_ref[...], preferred_element_type=F32)
+    mixed += jnp.dot(new.astype(BF16), nv_ref[...], preferred_element_type=F32)
+    o_ref[...] = (mixed / total).astype(BF16)
+
+
+def attend(cache_len, q, ck, cv, nk, nv):
+    rows, width = q.shape
+    return pl.pallas_call(
+        functools.partial(attend_kernel, seq_devs=KVH),
+        grid=(width // HD,),
+        out_shape=jax.ShapeDtypeStruct((rows, width), BF16),
+        in_specs=[
+            pl.BlockSpec(memory_space=pltpu.SMEM),
+            pl.BlockSpec((rows, HD), lambda h: (0, h)),
+            pl.BlockSpec(ck.shape, lambda h: (0, 0)),
+            pl.BlockSpec(cv.shape, lambda h: (0, 0)),
+            pl.BlockSpec(nk.shape, lambda h: (0, 0)),
+            pl.BlockSpec(nv.shape, lambda h: (0, 0)),
+        ],
+        out_specs=pl.BlockSpec((rows, HD), lambda h: (0, h)),
+        compiler_params=pltpu.CompilerParams(vmem_limit_bytes=40 << 20),
+    )(cache_len, q, ck, cv, nk, nv)
+
+
+def remote(src, dst, send, recv, dev):
+    return pltpu.make_async_remote_copy(
+        src_ref=src,
+        dst_ref=dst,
+        send_sem=send,
+        recv_sem=recv,
+        device_id={"ea": dev},
+        device_id_type=pl.DeviceIdType.MESH,
+    )
+
+
+def greet(me):
+    barrier = pltpu.get_barrier_semaphore()
+
+    def hello(off, carry):
+        pl.semaphore_signal(
+            barrier,
+            inc=1,
+            device_id={"ea": lax.rem(me + off, NDEV)},
+            device_id_type=pl.DeviceIdType.MESH,
+        )
+        return carry
+
+    lax.fori_loop(1, NDEV, hello, 0)
+    pl.semaphore_wait(barrier, NDEV - 1)
+
+
+def others(me, step):
+    def go(off, carry):
+        step(lax.rem(me + off, NDEV))
+        return carry
+
+    lax.fori_loop(1, NDEV, go, 0)
+
+
+def front_kernel(
+    att_ref, proj_ref, hid_ref, gain_ref, router_ref, ids_ref,
+    res_ref, gate_ref, place_ref, main_ref, extra_ref,
+    buf, acc, hs, arrived, normed, send_main, send_extra,
+    block_sem, left_sem, right_sem, y_sem, core_sem,
+    hs_send, hs_recv, main_send, main_recv, extra_send, extra_recv,
+):
+    me = lax.axis_index("ea")
+    z, y, c = me // 4, (me // 2) % 2, me % 2
+
+    def index(zz, yy, cc):
+        return (zz * 2 + yy) * 2 + cc
+
+    buf[me] = att_ref[...]
+    acc[...] = jnp.zeros_like(acc)
+    greet(me)
+
+    def block_copy(blk, sem, dev):
+        return remote(buf.at[blk], buf.at[blk], sem, block_sem.at[blk], dev)
+
+    def to_left(zz):
+        return block_copy(index(zz, y, c), left_sem.at[zz], index(z - 1, y, c))
+
+    def to_right(zz):
+        return block_copy(index(zz, y, c), right_sem.at[zz], index(z + 1, y, c))
+
+    def to_y(zz):
+        return block_copy(index(zz, y, c), y_sem.at[zz], index(z, 1 - y, c))
+
+    def to_core(zz, yy):
+        return block_copy(index(zz, yy, c), core_sem.at[zz * 2 + yy], index(z, y, 1 - c))
+
+    def landed(blk):
+        remote(buf.at[blk], buf.at[blk], left_sem.at[0], block_sem.at[blk], index(z, y, 1 - c)).wait_recv()
+
+    def line(zz, go_left, go_right):
+        if go_left:
+            @pl.when(z > 0)
+            def _():
+                to_left(zz).start()
+        if go_right:
+            @pl.when(z < NZ - 1)
+            def _():
+                to_right(zz).start()
+        to_y(zz).start()
+        to_core(zz, y).start()
+
+    def pair(d, step):
+        @pl.when(z + d < NZ)
+        def _():
+            step(z + d, True)
+
+        @pl.when(z - d >= 0)
+        def _():
+            step(z - d, False)
+
+    def arrive_line(d):
+        def step(zz, from_right):
+            landed(index(zz, y, c))
+            line(zz, from_right, not from_right)
+
+        pair(d, step)
+
+    def across(zz):
+        landed(index(zz, 1 - y, c))
+        to_core(zz, 1 - y).start()
+
+    def arrive_y(d):
+        if d == 0:
+            across(z)
+        else:
+            pair(d, lambda zz, _: across(zz))
+
+    def multiply(d):
+        def go(n, carry):
+            side, yy, cc = n % 2, (n // 2) % 2, n // 4
+            zz = z + d * (1 - 2 * side)
+            ok = (zz >= 0) & (zz < NZ)
+            if d == 0:
+                ok = ok & (side == 0)
+
+            @pl.when(ok)
+            def _():
+                blk = index(zz, (y + yy) % 2, (c + cc) % 2)
+
+                @pl.when(cc == 1)
+                def _():
+                    landed(blk)
+
+                group = blk % KVH
+                width = buf.shape[2]
+                rows = pl.ds(pl.multiple_of(group * width, width), width)
+                acc[blk // KVH] += jnp.dot(
+                    buf[blk], proj_ref[rows, :], preferred_element_type=F32
+                )
+
+            return carry
+
+        lax.fori_loop(0, 8, go, 0)
+
+    line(z, True, True)
+
+    ids = ids_ref[...]
+    lanes = lax.broadcasted_iota(jnp.int32, (ids.shape[0], EXPERTS), 1)
+    count = ids.shape[0]
+    first = (ids[:, 0:1] == lanes).astype(F32)
+    second = (ids[:, 1:2] == lanes).astype(F32)
+    tri = (
+        lax.broadcasted_iota(jnp.int32, (count, count), 1)
+        < lax.broadcasted_iota(jnp.int32, (count, count), 0)
+    ).astype(F32)
+    before0 = jnp.dot(tri, first, preferred_element_type=F32)
+    before1 = jnp.dot(tri, second, preferred_element_type=F32) + jnp.sum(
+        first, axis=0, keepdims=True
+    )
+    slot_lanes = lax.broadcasted_iota(jnp.int32, (count, SLOTS), 1).astype(F32)
+
+    def placing(before, one_hot, col):
+        slot = jnp.sum(before * one_hot, axis=1, keepdims=True)
+        expert = ids[:, col : col + 1].astype(F32)
+        where = jnp.where(slot < MAIN - 0.5, expert * MAIN + slot, EXPERTS * MAIN + expert)
+        return (slot_lanes == where).astype(F32)
+
+    place0 = placing(before0, first, 0)
+    place1 = placing(before1, second, 1)
+    place_ref[0] = place0.astype(BF16)
+    place_ref[1] = place1.astype(BF16)
+
+    for d in range(1, NZ):
+        arrive_line(d)
+        arrive_y(d - 1)
+        multiply(d - 1)
+    arrive_y(NZ - 1)
+    multiply(NZ - 1)
+
+    hs[...] = acc[...].astype(BF16)
+    piece = arrived.shape[1]
+    width = hs.shape[2]
+    col_me = pl.ds(pl.multiple_of(me * width, width), width)
+    row_me = pl.ds(pl.multiple_of(me * piece, piece), piece)
+
+    def hs_copy(dev):
+        rows = pl.ds(pl.multiple_of(dev * piece, piece), piece)
+        return remote(
+            hs.at[:, rows, :], arrived.at[:, :, col_me], hs_send.at[dev], hs_recv.at[me], dev
+        )
+
+    def hs_landed(dev):
+        cols = pl.ds(pl.multiple_of(dev * width, width), width)
+        remote(
+            hs.at[:, row_me, :], arrived.at[:, :, cols], hs_send.at[dev], hs_recv.at[dev], dev
+        ).wait_recv()
+
+    others(me, lambda dev: hs_copy(dev).start())
+    arrived[:, :, col_me] = hs[:, row_me, :]
+    others(me, hs_landed)
+
+    total = arrived[...].astype(F32).reshape(res_ref.shape)
+    residual = hid_ref[...].astype(F32) + total
+    res_ref[...] = residual
+    mean_sq = jnp.mean(residual * residual, axis=1, keepdims=True)
+    normed[...] = (residual * lax.rsqrt(mean_sq + 1e-05) * gain_ref[...]).astype(BF16)
+    select = (place0 + place1).T.astype(BF16)
+    packed = jnp.dot(select, normed[...], preferred_element_type=F32)
+    model = packed.shape[1]
+    send_main[...] = packed[: EXPERTS * MAIN].astype(BF16).reshape(NDEV, MAIN, model)
+    send_extra[...] = packed[EXPERTS * MAIN :].reshape(NDEV, 1, model)
+
+    def main_copy(src, dst, dev):
+        return remote(send_main.at[dev], main_ref.at[src], main_send.at[dev], main_recv.at[src], dev)
+
+    def extra_copy(src, dst, dev):
+        return remote(
+            send_extra.at[dev], extra_ref.at[src], extra_send.at[dev], extra_recv.at[src], dev
+        )
+
+    def dispatch(dev):
+        main_copy(me, dev, dev).start()
+        extra_copy(me, dev, dev).start()
+
+    others(me, dispatch)
+    main_ref[me] = send_main[me]
+    extra_ref[me] = send_extra[me]
+    logits = jnp.dot(normed[...], router_ref[...], preferred_element_type=F32)
+    gap = jnp.sum(logits * first, axis=1, keepdims=True) - jnp.sum(
+        logits * second, axis=1, keepdims=True
+    )
+    gate_ref[...] = jnp.broadcast_to(jax.nn.sigmoid(gap), gate_ref.shape)
+
+    def finish(dev):
+        main_copy(dev, me, dev).wait_recv()
+        extra_copy(dev, me, dev).wait_recv()
+        main_copy(me, dev, dev).wait_send()
+        extra_copy(me, dev, dev).wait_send()
+        hs_copy(dev).wait_send()
+
+    others(me, finish)
+    for zz in range(NZ):
+        @pl.when((z > 0) & (zz >= z))
+        def _():
+            to_left(zz).wait_send()
+
+        @pl.when((z < NZ - 1) & (zz <= z))
+        def _():
+            to_right(zz).wait_send()
+
+        to_y(zz).wait_send()
+        to_core(zz, 0).wait_send()
+        to_core(zz, 1).wait_send()
+
+
+def vmem(count):
+    return [pl.BlockSpec(memory_space=pltpu.VMEM)] * count
+
+
+def front(attended, out_proj, hidden, gain, router, ids):
+    rows, width = attended.shape
+    seqs = NDEV // KVH
+    cols = out_proj.shape[1]
+    mine, model = hidden.shape
+    dma = pltpu.SemaphoreType.DMA
+    return pl.pallas_call(
+        front_kernel,
+        out_shape=[
+            jax.ShapeDtypeStruct((mine, model), F32),
+            jax.ShapeDtypeStruct((mine, 128), F32),
+            jax.ShapeDtypeStruct((2, mine, SLOTS), BF16),
+            jax.ShapeDtypeStruct((NDEV, MAIN, model), BF16),
+            jax.ShapeDtypeStruct((NDEV, 1, model), F32),
+        ],
+        in_specs=vmem(6),
+        out_specs=vmem(5),
+        scratch_shapes=[
+            pltpu.VMEM((NDEV, rows, width), BF16),
+            pltpu.VMEM((seqs, rows, cols), F32),
+            pltpu.VMEM((seqs, rows, cols), BF16),
+            pltpu.VMEM((seqs, rows // NDEV, model), BF16),
+            pltpu.VMEM((mine, model), BF16),
+            pltpu.VMEM((NDEV, MAIN, model), BF16),
+            pltpu.VMEM((NDEV, 1, model), F32),
+            dma((NDEV,)), dma((NZ,)), dma((NZ,)), dma((NZ,)), dma((2 * NZ,)),
+            dma((NDEV,)), dma((NDEV,)), dma((NDEV,)), dma((NDEV,)), dma((NDEV,)), dma((NDEV,)),
+        ],
+        compiler_params=pltpu.CompilerParams(
+            collective_id=0, has_side_effects=True, vmem_limit_bytes=50 << 20
+        ),
+    )(attended, out_proj, hidden, gain, router, ids)
+
+
+def expert_kernel(main_ref, extra_ref, gate_ref, up_ref, down_ref, omain_ref, oextra_ref, x, acc):
+    step = pl.program_id(0)
+    cut = EXPERTS * MAIN
+
+    @pl.when(step == 0)
+    def _():
+        x[:cut] = main_ref[...].reshape(cut, x.shape[1])
+        x[cut:] = extra_ref[...].reshape(EXPERTS, x.shape[1]).astype(BF16)
+        acc[...] = jnp.zeros_like(acc)
+
+    gate = jnp.dot(x[...], gate_ref[...], preferred_element_type=F32)
+    up = jnp.dot(x[...], up_ref[...], preferred_element_type=F32)
+    inner = (gate / (1.0 + jnp.exp(-gate)) * up).astype(BF16)
+    acc[...] += jnp.dot(inner, down_ref[...], preferred_element_type=F32)
+
+    @pl.when(step == pl.num_programs(0) - 1)
+    def _():
+        omain_ref[...] = acc[:cut].astype(BF16).reshape(omain_ref.shape)
+        oextra_ref[...] = acc[cut:].astype(BF16).astype(F32).reshape(oextra_ref.shape)
+
+
+def experts(main, extra, gate_proj, up_proj, down_proj):
+    model, hidden = gate_proj.shape
+    tile = 640
+    zero3 = lambda i: (0, 0, 0)
+    return pl.pallas_call(
+        expert_kernel,
+        grid=(hidden // tile,),
+        out_shape=[
+            jax.ShapeDtypeStruct(main.shape, BF16),
+            jax.ShapeDtypeStruct(extra.shape, F32),
+        ],
+        in_specs=[
+            pl.BlockSpec(main.shape, zero3),
+            pl.BlockSpec(extra.shape, zero3),
+            pl.BlockSpec((model, tile), lambda i: (0, i)),
+            pl.BlockSpec((model, tile), lambda i: (0, i)),
+            pl.BlockSpec((tile, model), lambda i: (i, 0)),
+        ],
+        out_specs=[pl.BlockSpec(main.shape, zero3), pl.BlockSpec(extra.shape, zero3)],
+        scratch_shapes=[pltpu.VMEM((SLOTS, model), BF16), pltpu.VMEM((SLOTS, model), F32)],
+        compiler_params=pltpu.CompilerParams(vmem_limit_bytes=56 << 20),
+    )(main, extra, gate_proj, up_proj, down_proj)
+
+
+def back_kernel(
+    main_ref, extra_ref, res_ref, gate_ref, place_ref, out_ref,
+    got_main, got_extra, terms, main_send, main_recv, extra_send, extra_recv,
+):
+    me = lax.axis_index("ea")
+    greet(me)
+
+    def main_copy(src, dev):
+        return remote(main_ref.at[dev], got_main.at[src], main_send.at[dev], main_recv.at[src], dev)
+
+    def extra_copy(src, dev):
+        return remote(
+            extra_ref.at[dev], got_extra.at[src], extra_send.at[dev], extra_recv.at[src], dev
+        )
+
+    def start(dev):
+        main_copy(me, dev).start()
+        extra_copy(me, dev).start()
+
+    others(me, start)
+    got_main[me] = main_ref[me]
+    got_extra[me] = extra_ref[me]
+
+    def finish(dev):
+        main_copy(dev, dev).wait_recv()
+        extra_copy(dev, dev).wait_recv()
+        main_copy(me, dev).wait_send()
+        extra_copy(me, dev).wait_send()
+
+    others(me, finish)
+    cut = EXPERTS * MAIN
+    model = terms.shape[1]
+    terms[:cut] = got_main[...].reshape(cut, model)
+    terms[cut:] = got_extra[...].reshape(EXPERTS, model).astype(BF16)
+    gate0 = gate_ref[:, 0:1]
+    pick0 = jnp.dot(place_ref[0], terms[...], preferred_element_type=F32)
+    pick1 = jnp.dot(place_ref[1], terms[...], preferred_element_type=F32)
+    mixed = res_ref[...] + gate0 * pick0 + (1.0 - gate0) * pick1
+    out_ref[...] = mixed.astype(BF16)
+
+
+def back(main, extra, residual, gate, place):
+    dma = pltpu.SemaphoreType.DMA
+    return pl.pallas_call(
+        back_kernel,
+        out_shape=jax.ShapeDtypeStruct(residual.shape, BF16),
+        in_specs=vmem(5),
+        out_specs=vmem(1)[0],
+        scratch_shapes=[
+            pltpu.VMEM(main.shape, BF16),
+            pltpu.VMEM(extra.shape, F32),
+            pltpu.VMEM((SLOTS, residual.shape[1]), BF16),
+            dma((NDEV,)), dma((NDEV,)), dma((NDEV,)), dma((NDEV,)),
+        ],
+        compiler_params=pltpu.CompilerParams(
+            collective_id=1, has_side_effects=True, vmem_limit_bytes=40 << 20
+        ),
+    )(main, extra, residual, gate, place)
+
+
+def body(
+    hidden_in, queries, cache_keys, cache_values, new_keys, new_values, cache_len,
+    out_proj, norm_gain, router, expert_ids, gate_proj, up_proj, down_proj,
+):
+    piece, seqs, model = hidden_in.shape
+    attended = attend(
+        cache_len, queries[0], cache_keys[0], cache_values[0], new_keys[0], new_values[0]
+    )
+    hidden = hidden_in.transpose(1, 0, 2).reshape(piece * seqs, model)
+    ids = expert_ids.transpose(1, 0, 2).reshape(piece * seqs, TOPK)
+    residual, gate, place, main, extra = front(
+        attended, out_proj, hidden, norm_gain.reshape(1, model), router, ids
+    )
+    main, extra = experts(main, extra, gate_proj, up_proj, down_proj)
+    out = back(main, extra, residual, gate, place)
+    return out.reshape(seqs, piece, model).transpose(1, 0, 2)
+
+
 def solution(mesh):
     placed = (
         P("ea", "rep", None),
@@ -174,6 +635,7 @@
         P(None, "ea"),
         P("ea", None),
     )
+    plan = body if mesh.shape["ea"] == NDEV else wide_body
     return jax.shard_map(
-        body, mesh=mesh, in_specs=placed, out_specs=P("ea", "rep", None), check_vma=False
-    )
+        plan, mesh=mesh, in_specs=placed, out_specs=P("ea", "rep", None), check_vma=False
+    )

time: 379 us -> 186 us (0.49)
  waiting for transfers between devices: 197 us -> 0 us
  Pallas kernels: 0 us -> 169 us
  matrix products: 81.4 us -> 0 us
  starting transfers between devices: 37.6 us -> 0 us
  local copies, waits for them, and re-layouts: 48.6 us -> 15.5 us
  other arithmetic: 13.3 us -> 0 us
    all_to_all x6 -> x0, waiting for transfers between devices: 197 us -> none  [the longest x1 88.8 us: body(): lax.all_to_all(head_part.reshape(piece_rows, dev_count, model_width), 'ea...]
    pallas_call x0 -> x4, Pallas kernels: none -> 169 us  [the longest x1 99.6 us: front(): pl.pallas_call(front_kernel, out_shape=[jax.ShapeDtypeStruct((mine, model...]
    dot_general x9 -> x0, matrix products: 75.1 us -> none  [the longest x2 39.9 us: expert_terms(): jnp.dot(inner_act, down_proj, preferred_element_type=jnp.float32)]
    all_to_all x6 -> x0, starting transfers between devices: 37.6 us -> none  [the longest x2 12.1 us: expert_half(): lax.all_to_all(shard_term, 'ea', split_axis=0, concat_axis=0, tiled=True)]
    unnamed x28 -> x23, local copies, waits for them, and re-layouts: 0.48 us -> 12.1 us
    reshape x9 -> x2, local copies, waits for them, and re-layouts: 11.1 us -> 2.1 us  [the longest x1 1.34 us: body(): return out.reshape(seqs, piece, model).transpose(1, 0, 2)]
    gather x7 -> x0, local copies, waits for them, and re-layouts: 6.79 us -> none  [the longest x2 5.04 us: route_rows(): picked = jnp.take(expert_out, target, axis=0)]
    all_to_all x1 -> x0, local copies, waits for them, and re-layouts: 6.41 us -> none  [body(): lax.all_to_all(outgoing, 'ea', split_axis=1, concat_axis=1, tiled=True)]
  transfers between devices with their start and end apart: 6 -> 0, of which waited for: 4 -> 0; matrix products, arithmetic and copies ran while one was open for 24% -> 0% of each run, Pallas kernels for 0% -> 0%
where the time goes in v1:
time: 186 us; the launch traced here: 185 us
  Pallas kernels  169 us (91%)
  local copies, waits for them, and re-layouts  15.5 us (8%)
    pallas_call x1, Pallas kernels, front(): pl.pallas_call(front_kernel, out_shape=[jax.ShapeDtypeStruct((mine, model...  99.6 us
    pallas_call x1, Pallas kernels, back(): pl.pallas_call(back_kernel, out_shape=jax.ShapeDtypeStruct(residual.shape...  33.4 us
    pallas_call x1, Pallas kernels, experts(): pl.pallas_call(expert_kernel, grid=(hidden // tile,), out_shape=[jax.Shap...  29.8 us
    unnamed x23, local copies, waits for them, and re-layouts  12.1 us
    pallas_call x1, Pallas kernels, attend(): pl.pallas_call(functools.partial(attend_kernel, seq_devs=KVH), grid=(widt...  6.27 us

profile of v1, /device:TPU:9, one launch (start us, length us, event | category | flops | bytes accessed | tf_op | source)
XLA Modules:
  0.0 184.7 jit_solution(10741570170771677153)
XLA Ops:
  0.0 0.8 copy.20
  0.8 1.3 copy.15
  2.1 0.0 copy-start.2
  2.1 1.0 copy-done.2
  3.2 0.0 copy-start.5
  3.2 0.9 copy-done.5
  4.1 0.0 copy-start.6
  4.1 0.9 copy-done.6
  5.0 0.0 copy-start.7
  5.0 0.9 copy-done.7
  5.9 0.0 copy-start.8
  5.9 0.9 copy-done.8
  6.8 0.0 copy-start.10
  6.8 0.7 copy-done.10
  7.4 6.3 %shard_map.136.att_ref = bf16[512,512]{1,0:T(8,128)(2,1)S(1)} custom-call(s32[2]{0:T(128)S(1)} %copy-done.10, bf16[512,512]{1,0:T(8,128)(2,1)S(1)} %bitcast.16, bf16[512,128]{1,0:T(8,128)(2,1)S(1)} %bitcast.18, bf16[512,128]{1,0:T(8,128)(2,1)S(1)} %bitcast.19, bf16[512,128]{1,0:T(8,128)(2,1)S(1)} %bitcast.20, bf16[512,128]{1,0:T(8,128)(2,1)S(1)} %bitcast.21), custom_call_target="tpu_custom_call" | custom-call | tf_op jit(solution)/shard_map/pallas_call | solution.py:197
  13.7 2.2 %copy.17.router_ref = bf16[4096,16]{1,0:T(8,128)(2,1)} copy(bf16[4096,16]{0,1:T(8,128)(2,1)} %param.23) | data formatting | bytes 262144 | tf_op args[9]
  15.9 0.0 copy-start.9
  15.9 0.7 copy-done.9
  16.6 99.6 %shard_map.137 = (f32[64,4096]{1,0:T(8,128)S(1)}, f32[64,128]{1,0:T(8,128)S(1)}, bf16[2,64,144]{2,1,0:T(8,128)(2,1)S(1)}, bf16[16,8,4096]{2,1,0:T(8,128)(2,1)S(1)}, f32[16,1,4096]{2,1,0:T(1,128)S(1)}) custom-call(bf16[512,512]{1,0:T(8,128)(2,1)S(1)} %shard_map.136.att_ref, bf16[4096,256]{1,0:T(8,128)(2,1)} %proj_ref.1, bf16[64,4096]{1,0:T(8,128)(2,1)S(1)} %bitcast.15, ...), custom_call_target="tpu_custom_call" | custom-call | tf_op jit(solution)/shard_map/pallas_call | solution.py:470
  116.2 0.0 copy-start
  116.2 1.0 copy-done
  117.2 0.0 copy-start.3
  117.2 0.7 copy-done.3
  117.9 29.8 %shard_map.138 = (bf16[16,8,4096]{2,1,0:T(8,128)(2,1)}, f32[16,1,4096]{2,1,0:T(1,128)}) custom-call(bf16[16,8,4096]{2,1,0:T(8,128)(2,1)} %copy-done, f32[16,1,4096]{2,1,0:T(1,128)} %copy-done.3, bf16[4096,3200]{1,0:T(8,128)(2,1)} %gate_ref.1, bf16[4096,3200]{1,0:T(8,128)(2,1)} %up_ref.1, bf16[3200,4096]{1,0:T(8,128)(2,1)} %down_ref.1), custom_call_target="tpu_custom_call" | custom-call | tf_op jit(solution)/shard_map/pallas_call | solution.py:523
  147.7 0.0 copy-start.1
  147.7 1.2 copy-done.1
  149.0 0.0 copy-start.4
  149.0 0.9 copy-done.4
  149.9 33.4 %shard_map.139 = bf16[64,4096]{1,0:T(8,128)(2,1)S(1)} custom-call(bf16[16,8,4096]{2,1,0:T(8,128)(2,1)S(1)} %copy-done.1, f32[16,1,4096]{2,1,0:T(1,128)S(1)} %copy-done.4, f32[64,4096]{1,0:T(8,128)S(1)} %get-tuple-element.16.res_ref, f32[64,128]{1,0:T(8,128)S(1)} %get-tuple-element.17.gate_ref, bf16[2,64,144]{2,1,0:T(8,128)(2,1)S(1)} %get-tuple-element.18.place_ref), custom_call_target="tpu_custom_call" | custom-call | tf_op jit(solution)/shard_map/pallas_call | solution.py:586
  183.4 1.3 copy.23
Async XLA Ops:
  2.1 1.0 copy-start.2
  3.2 0.9 copy-start.5
  4.1 0.9 copy-start.6
  5.0 0.9 copy-start.7
  5.9 0.9 copy-start.8
  6.8 0.7 copy-start.10
  15.9 0.7 copy-start.9
  116.2 1.0 copy-start
  117.2 0.7 copy-start.3
  147.7 1.2 copy-start.1
  149.0 0.9 copy-start.4

commit v2 on v1

--- a/solution.py
+++ b/solution.py
@@ -246,19 +246,56 @@
     lax.fori_loop(1, NDEV, go, 0)
 
 
-def front_kernel(
-    att_ref, proj_ref, hid_ref, gain_ref, router_ref, ids_ref,
-    res_ref, gate_ref, place_ref, main_ref, extra_ref,
-    buf, acc, hs, arrived, normed, send_main, send_extra,
+TILE = 640
+TILES = 5
+GU_SLOTS = 3
+DN_SLOTS = 2
+BACK = 1024
+
+
+def layer_kernel(
+    att_ref, proj_hbm, hid_hbm, gain_ref, router_hbm, ids_ref, gate_hbm, up_hbm, down_hbm,
+    out_ref,
+    buf, acc, hs, arrived, normed, proj_ref, hid_ref, router_ref, res_ref, gate_ref, place_ref,
+    out_go, out_got, x, gacc, uacc, inner, back_go, back_got, fold, fold_back, terms, gu, dn,
+    in_sem, gu_sem, dn_sem,
     block_sem, left_sem, right_sem, y_sem, core_sem,
-    hs_send, hs_recv, main_send, main_recv, extra_send, extra_recv,
+    hs_send, hs_recv, go_send, go_recv, back_send, back_recv,
 ):
     me = lax.axis_index("ea")
+    half = x.shape[2]
+    cut = EXPERTS * MAIN
     z, y, c = me // 4, (me // 2) % 2, me % 2
 
     def index(zz, yy, cc):
         return (zz * 2 + yy) * 2 + cc
 
+    def fetch(src, dst, slot):
+        return pltpu.make_async_copy(src, dst, in_sem.at[slot])
+
+    loads = [(proj_hbm, proj_ref), (hid_hbm, hid_ref), (router_hbm, router_ref)]
+    for slot, (src, dst) in enumerate(loads):
+        fetch(src, dst, slot).start()
+
+    def gate_up(u):
+        h, t, slot = u // TILES, u % TILES, u % GU_SLOTS
+        rows = pl.ds(pl.multiple_of(h * half, half), half)
+        cols = pl.ds(pl.multiple_of(t * TILE, TILE), TILE)
+        return [
+            pltpu.make_async_copy(src.at[rows, cols], gu.at[slot, n], gu_sem.at[slot, n])
+            for n, src in enumerate((gate_hbm, up_hbm))
+        ]
+
+    def down(n):
+        cols = pl.ds(pl.multiple_of(n * BACK, BACK), BACK)
+        slot = n % DN_SLOTS
+        return pltpu.make_async_copy(down_hbm.at[:, cols], dn.at[slot], dn_sem.at[slot])
+
+    for u in range(GU_SLOTS):
+        for copy in gate_up(u):
+            copy.start()
+    for n in range(DN_SLOTS):
+        down(n).start()
     buf[me] = att_ref[...]
     acc[...] = jnp.zeros_like(acc)
     greet(me)
@@ -373,6 +410,7 @@
     place1 = placing(before1, second, 1)
     place_ref[0] = place0.astype(BF16)
     place_ref[1] = place1.astype(BF16)
+    fetch(proj_hbm, proj_ref, 0).wait()
 
     for d in range(1, NZ):
         arrive_line(d)
@@ -403,44 +441,129 @@
     arrived[:, :, col_me] = hs[:, row_me, :]
     others(me, hs_landed)
 
+    fetch(hid_hbm, hid_ref, 1).wait()
+    fetch(router_hbm, router_ref, 2).wait()
     total = arrived[...].astype(F32).reshape(res_ref.shape)
     residual = hid_ref[...].astype(F32) + total
     res_ref[...] = residual
     mean_sq = jnp.mean(residual * residual, axis=1, keepdims=True)
     normed[...] = (residual * lax.rsqrt(mean_sq + 1e-05) * gain_ref[...]).astype(BF16)
     select = (place0 + place1).T.astype(BF16)
-    packed = jnp.dot(select, normed[...], preferred_element_type=F32)
-    model = packed.shape[1]
-    send_main[...] = packed[: EXPERTS * MAIN].astype(BF16).reshape(NDEV, MAIN, model)
-    send_extra[...] = packed[EXPERTS * MAIN :].reshape(NDEV, 1, model)
-
-    def main_copy(src, dst, dev):
-        return remote(send_main.at[dev], main_ref.at[src], main_send.at[dev], main_recv.at[src], dev)
-
-    def extra_copy(src, dst, dev):
+
+    def pack(store, fold_ref, values, wide):
+        part = wide // MAIN
+        for q in range(MAIN):
+            fold_ref[:, q, :] = values[cut:, q * part : (q + 1) * part]
+        store[:, :, :wide] = values[:cut].astype(BF16).reshape(NDEV, MAIN, wide)
+        store[:, :, wide:] = fold_ref[...].astype(BF16)
+
+    def unpack(store, fold_ref, place, wide):
+        part = wide // MAIN
+        place[:cut] = store[:, :, :wide].reshape(cut, wide)
+        fold_ref[...] = store[:, :, wide:].astype(F32)
+        for q in range(MAIN):
+            place[cut:, q * part : (q + 1) * part] = fold_ref[:, q, :].astype(BF16)
+
+    def go_copy(h, src, dev):
         return remote(
-            send_extra.at[dev], extra_ref.at[src], extra_send.at[dev], extra_recv.at[src], dev
+            out_go.at[h, dev], out_got.at[h, src], go_send.at[h, dev], go_recv.at[h, src], dev
         )
 
-    def dispatch(dev):
-        main_copy(me, dev, dev).start()
-        extra_copy(me, dev, dev).start()
-
-    others(me, dispatch)
-    main_ref[me] = send_main[me]
-    extra_ref[me] = send_extra[me]
-    logits = jnp.dot(normed[...], router_ref[...], preferred_element_type=F32)
+    def back_copy(n, src, dev):
+        return remote(
+            back_go.at[n, dev], back_got.at[n, src], back_send.at[n, dev], back_recv.at[n, src], dev
+        )
+
+    for h in range(2):
+        packed = jnp.dot(
+            select, normed[:, h * half : (h + 1) * half], preferred_element_type=F32
+        )
+        pack(out_go.at[h], fold, packed, half)
+        others(me, lambda dev: go_copy(h, me, dev).start())
+        out_got[h, me] = out_go[h, me]
+
+    logits = lax.dot_general(
+        normed[...], router_ref[...], (((1,), (1,)), ((), ())), preferred_element_type=F32
+    )
     gap = jnp.sum(logits * first, axis=1, keepdims=True) - jnp.sum(
         logits * second, axis=1, keepdims=True
     )
     gate_ref[...] = jnp.broadcast_to(jax.nn.sigmoid(gap), gate_ref.shape)
 
+    for h in range(2):
+        others(me, lambda dev: go_copy(h, dev, dev).wait_recv())
+        unpack(out_got.at[h], fold, x.at[h], half)
+
+        def tile_step(t, carry):
+            u = h * TILES + t
+            slot = u % GU_SLOTS
+            for copy in gate_up(u):
+                copy.wait()
+            gate = jnp.dot(x[h], gu[slot, 0], preferred_element_type=F32)
+            up = jnp.dot(x[h], gu[slot, 1], preferred_element_type=F32)
+            if h == 0:
+                gacc[t] = gate
+                uacc[t] = up
+            else:
+                gate = gacc[t] + gate
+                up = uacc[t] + up
+                cols = pl.ds(pl.multiple_of(t * TILE, TILE), TILE)
+                inner[:, cols] = (gate / (1.0 + jnp.exp(-gate)) * up).astype(BF16)
+
+            @pl.when(u + GU_SLOTS < 2 * TILES)
+            def _():
+                for copy in gate_up(u + GU_SLOTS):
+                    copy.start()
+
+            return carry
+
+        lax.fori_loop(0, TILES, tile_step, 0)
+
+    chunks = back_go.shape[0]
+
+    def down_step(n, carry):
+        down(n).wait()
+        pack(
+            back_go.at[n],
+            fold_back,
+            jnp.dot(inner[...], dn[n % DN_SLOTS], preferred_element_type=F32),
+            BACK,
+        )
+        others(me, lambda dev: back_copy(n, me, dev).start())
+        back_got[n, me] = back_go[n, me]
+
+        @pl.when(n + DN_SLOTS < chunks)
+        def _():
+            down(n + DN_SLOTS).start()
+
+        return carry
+
+    lax.fori_loop(0, chunks, down_step, 0)
+
+    gate0 = gate_ref[:, 0:1]
+
+    def combine(n, carry):
+        others(me, lambda dev: back_copy(n, dev, dev).wait_recv())
+        unpack(back_got.at[n], fold_back, terms, BACK)
+        cols = pl.ds(pl.multiple_of(n * BACK, BACK), BACK)
+        pick0 = jnp.dot(place_ref[0], terms[...], preferred_element_type=F32)
+        pick1 = jnp.dot(place_ref[1], terms[...], preferred_element_type=F32)
+        mixed = res_ref[:, cols] + gate0 * pick0 + (1.0 - gate0) * pick1
+        out_ref[:, cols] = mixed.astype(BF16)
+        return carry
+
+    lax.fori_loop(0, chunks, combine, 0)
+
     def finish(dev):
-        main_copy(dev, me, dev).wait_recv()
-        extra_copy(dev, me, dev).wait_recv()
-        main_copy(me, dev, dev).wait_send()
-        extra_copy(me, dev, dev).wait_send()
         hs_copy(dev).wait_send()
+        for h in range(2):
+            go_copy(h, me, dev).wait_send()
+
+        def sent(n, carry):
+            back_copy(n, me, dev).wait_send()
+            return carry
+
+        lax.fori_loop(0, chunks, sent, 0)
 
     others(me, finish)
     for zz in range(NZ):
@@ -457,147 +580,57 @@
         to_core(zz, 1).wait_send()
 
 
-def vmem(count):
-    return [pl.BlockSpec(memory_space=pltpu.VMEM)] * count
-
-
-def front(attended, out_proj, hidden, gain, router, ids):
+def layer(attended, out_proj, hidden, gain, router, ids, gate_proj, up_proj, down_proj):
     rows, width = attended.shape
     seqs = NDEV // KVH
     cols = out_proj.shape[1]
     mine, model = hidden.shape
+    ffw = gate_proj.shape[1]
+    half, chunks = model // 2, model // BACK
     dma = pltpu.SemaphoreType.DMA
+    inside = pl.BlockSpec(memory_space=pltpu.VMEM)
+    outside = pl.BlockSpec(memory_space=pl.ANY)
+    go = (2, NDEV, MAIN, half + half // MAIN)
+    back = (chunks, NDEV, MAIN, BACK + BACK // MAIN)
     return pl.pallas_call(
-        front_kernel,
-        out_shape=[
-            jax.ShapeDtypeStruct((mine, model), F32),
-            jax.ShapeDtypeStruct((mine, 128), F32),
-            jax.ShapeDtypeStruct((2, mine, SLOTS), BF16),
-            jax.ShapeDtypeStruct((NDEV, MAIN, model), BF16),
-            jax.ShapeDtypeStruct((NDEV, 1, model), F32),
-        ],
-        in_specs=vmem(6),
-        out_specs=vmem(5),
+        layer_kernel,
+        out_shape=jax.ShapeDtypeStruct((mine, model), BF16),
+        in_specs=[inside, outside, outside, inside, outside, inside] + [outside] * 3,
+        out_specs=inside,
         scratch_shapes=[
             pltpu.VMEM((NDEV, rows, width), BF16),
             pltpu.VMEM((seqs, rows, cols), F32),
             pltpu.VMEM((seqs, rows, cols), BF16),
             pltpu.VMEM((seqs, rows // NDEV, model), BF16),
             pltpu.VMEM((mine, model), BF16),
-            pltpu.VMEM((NDEV, MAIN, model), BF16),
-            pltpu.VMEM((NDEV, 1, model), F32),
+            pltpu.VMEM(out_proj.shape, BF16),
+            pltpu.VMEM(hidden.shape, BF16),
+            pltpu.VMEM(router.shape, BF16),
+            pltpu.VMEM((mine, model), F32),
+            pltpu.VMEM((mine, 128), F32),
+            pltpu.VMEM((2, mine, SLOTS), BF16),
+            pltpu.VMEM(go, BF16),
+            pltpu.VMEM(go, BF16),
+            pltpu.VMEM((2, SLOTS, half), BF16),
+            pltpu.VMEM((TILES, SLOTS, TILE), F32),
+            pltpu.VMEM((TILES, SLOTS, TILE), F32),
+            pltpu.VMEM((SLOTS, ffw), BF16),
+            pltpu.VMEM(back, BF16),
+            pltpu.VMEM(back, BF16),
+            pltpu.VMEM((NDEV, MAIN, half // MAIN), F32),
+            pltpu.VMEM((NDEV, MAIN, BACK // MAIN), F32),
+            pltpu.VMEM((SLOTS, BACK), BF16),
+            pltpu.VMEM((GU_SLOTS, 2, half, TILE), BF16),
+            pltpu.VMEM((DN_SLOTS, ffw, BACK), BF16),
+            dma((3,)), dma((GU_SLOTS, 2)), dma((DN_SLOTS,)),
             dma((NDEV,)), dma((NZ,)), dma((NZ,)), dma((NZ,)), dma((2 * NZ,)),
-            dma((NDEV,)), dma((NDEV,)), dma((NDEV,)), dma((NDEV,)), dma((NDEV,)), dma((NDEV,)),
+            dma((NDEV,)), dma((NDEV,)), dma((2, NDEV)), dma((2, NDEV)),
+            dma((chunks, NDEV)), dma((chunks, NDEV)),
         ],
         compiler_params=pltpu.CompilerParams(
-            collective_id=0, has_side_effects=True, vmem_limit_bytes=50 << 20
+            collective_id=0, has_side_effects=True, vmem_limit_bytes=62 << 20
         ),
-    )(attended, out_proj, hidden, gain, router, ids)
-
-
-def expert_kernel(main_ref, extra_ref, gate_ref, up_ref, down_ref, omain_ref, oextra_ref, x, acc):
-    step = pl.program_id(0)
-    cut = EXPERTS * MAIN
-
-    @pl.when(step == 0)
-    def _():
-        x[:cut] = main_ref[...].reshape(cut, x.shape[1])
-        x[cut:] = extra_ref[...].reshape(EXPERTS, x.shape[1]).astype(BF16)
-        acc[...] = jnp.zeros_like(acc)
-
-    gate = jnp.dot(x[...], gate_ref[...], preferred_element_type=F32)
-    up = jnp.dot(x[...], up_ref[...], preferred_element_type=F32)
-    inner = (gate / (1.0 + jnp.exp(-gate)) * up).astype(BF16)
-    acc[...] += jnp.dot(inner, down_ref[...], preferred_element_type=F32)
-
-    @pl.when(step == pl.num_programs(0) - 1)
-    def _():
-        omain_ref[...] = acc[:cut].astype(BF16).reshape(omain_ref.shape)
-        oextra_ref[...] = acc[cut:].astype(BF16).astype(F32).reshape(oextra_ref.shape)
-
-
-def experts(main, extra, gate_proj, up_proj, down_proj):
-    model, hidden = gate_proj.shape
-    tile = 640
-    zero3 = lambda i: (0, 0, 0)
-    return pl.pallas_call(
-        expert_kernel,
-        grid=(hidden // tile,),
-        out_shape=[
-            jax.ShapeDtypeStruct(main.shape, BF16),
-            jax.ShapeDtypeStruct(extra.shape, F32),
-        ],
-        in_specs=[
-            pl.BlockSpec(main.shape, zero3),
-            pl.BlockSpec(extra.shape, zero3),
-            pl.BlockSpec((model, tile), lambda i: (0, i)),
-            pl.BlockSpec((model, tile), lambda i: (0, i)),
-            pl.BlockSpec((tile, model), lambda i: (i, 0)),
-        ],
-        out_specs=[pl.BlockSpec(main.shape, zero3), pl.BlockSpec(extra.shape, zero3)],
-        scratch_shapes=[pltpu.VMEM((SLOTS, model), BF16), pltpu.VMEM((SLOTS, model), F32)],
-        compiler_params=pltpu.CompilerParams(vmem_limit_bytes=56 << 20),
-    )(main, extra, gate_proj, up_proj, down_proj)
-
-
-def back_kernel(
-    main_ref, extra_ref, res_ref, gate_ref, place_ref, out_ref,
-    got_main, got_extra, terms, main_send, main_recv, extra_send, extra_recv,
-):
-    me = lax.axis_index("ea")
-    greet(me)
-
-    def main_copy(src, dev):
-        return remote(main_ref.at[dev], got_main.at[src], main_send.at[dev], main_recv.at[src], dev)
-
-    def extra_copy(src, dev):
-        return remote(
-            extra_ref.at[dev], got_extra.at[src], extra_send.at[dev], extra_recv.at[src], dev
-        )
-
-    def start(dev):
-        main_copy(me, dev).start()
-        extra_copy(me, dev).start()
-
-    others(me, start)
-    got_main[me] = main_ref[me]
-    got_extra[me] = extra_ref[me]
-
-    def finish(dev):
-        main_copy(dev, dev).wait_recv()
-        extra_copy(dev, dev).wait_recv()
-        main_copy(me, dev).wait_send()
-        extra_copy(me, dev).wait_send()
-
-    others(me, finish)
-    cut = EXPERTS * MAIN
-    model = terms.shape[1]
-    terms[:cut] = got_main[...].reshape(cut, model)
-    terms[cut:] = got_extra[...].reshape(EXPERTS, model).astype(BF16)
-    gate0 = gate_ref[:, 0:1]
-    pick0 = jnp.dot(place_ref[0], terms[...], preferred_element_type=F32)
-    pick1 = jnp.dot(place_ref[1], terms[...], preferred_element_type=F32)
-    mixed = res_ref[...] + gate0 * pick0 + (1.0 - gate0) * pick1
-    out_ref[...] = mixed.astype(BF16)
-
-
-def back(main, extra, residual, gate, place):
-    dma = pltpu.SemaphoreType.DMA
-    return pl.pallas_call(
-        back_kernel,
-        out_shape=jax.ShapeDtypeStruct(residual.shape, BF16),
-        in_specs=vmem(5),
-        out_specs=vmem(1)[0],
-        scratch_shapes=[
-            pltpu.VMEM(main.shape, BF16),
-            pltpu.VMEM(extra.shape, F32),
-            pltpu.VMEM((SLOTS, residual.shape[1]), BF16),
-            dma((NDEV,)), dma((NDEV,)), dma((NDEV,)), dma((NDEV,)),
-        ],
-        compiler_params=pltpu.CompilerParams(
-            collective_id=1, has_side_effects=True, vmem_limit_bytes=40 << 20
-        ),
-    )(main, extra, residual, gate, place)
+    )(attended, out_proj, hidden, gain, router, ids, gate_proj, up_proj, down_proj)
 
 
 def body(
@@ -610,11 +643,10 @@
     )
     hidden = hidden_in.transpose(1, 0, 2).reshape(piece * seqs, model)
     ids = expert_ids.transpose(1, 0, 2).reshape(piece * seqs, TOPK)
-    residual, gate, place, main, extra = front(
-        attended, out_proj, hidden, norm_gain.reshape(1, model), router, ids
-    )
-    main, extra = experts(main, extra, gate_proj, up_proj, down_proj)
-    out = back(main, extra, residual, gate, place)
+    out = layer(
+        attended, out_proj, hidden, norm_gain.reshape(1, model), router.T, ids,
+        gate_proj, up_proj, down_proj,
+    )
     return out.reshape(seqs, piece, model).transpose(1, 0, 2)
 
 

time: 186 us -> 152 us (0.82)
  Pallas kernels: 169 us -> 138 us
  local copies, waits for them, and re-layouts: 15.5 us -> 12 us
    pallas_call x3 -> x1, Pallas kernels: 163 us -> 132 us  [layer(): pl.pallas_call(layer_kernel, out_shape=jax.ShapeDtypeStruct((mine, model)...]
    unnamed x23 -> x14, local copies, waits for them, and re-layouts: 12.1 us -> 6.1 us
where the time goes in v2:
time: 152 us; the launch traced here: 150 us
  Pallas kernels  138 us (91%)
  local copies, waits for them, and re-layouts  12 us (8%)
    pallas_call x1, Pallas kernels, layer(): pl.pallas_call(layer_kernel, out_shape=jax.ShapeDtypeStruct((mine, model)...  132 us
    pallas_call x1, Pallas kernels, attend(): pl.pallas_call(functools.partial(attend_kernel, seq_devs=KVH), grid=(widt...  6.27 us
    unnamed x14, local copies, waits for them, and re-layouts  6.1 us

profile of v2, /device:TPU:9, one launch (start us, length us, event | category | flops | bytes accessed | tf_op | source)
XLA Modules:
  0.0 150.2 jit_solution(668904279865881691)
XLA Ops:
  0.0 1.4 copy.19
  1.4 2.1 %copy.15 = bf16[2,32,4096]{2,1,0:T(8,128)(2,1)} copy(bf16[2,32,4096]{2,0,1:T(2,128)(2,1)} %bitcast.22) | data formatting | bytes 1048576 | tf_op jit(solution)/shard_map/transpose | solution.py:644
  3.5 0.0 copy-start.1
  3.5 1.0 copy-done.1
  4.6 0.0 copy-start.2
  4.6 0.9 copy-done.2
  5.5 0.0 copy-start.3
  5.5 0.9 copy-done.3
  6.4 0.0 copy-start.4
  6.4 0.9 copy-done.4
  7.3 0.0 copy-start.5
  7.3 0.9 copy-done.5
  8.2 0.0 copy-start.6
  8.2 0.7 copy-done.6
  8.8 6.3 %shard_map.136.att_ref = bf16[512,512]{1,0:T(8,128)(2,1)S(1)} custom-call(s32[2]{0:T(128)S(1)} %copy-done.6, bf16[512,512]{1,0:T(8,128)(2,1)S(1)} %bitcast.15, bf16[512,128]{1,0:T(8,128)(2,1)S(1)} %bitcast.16, bf16[512,128]{1,0:T(8,128)(2,1)S(1)} %bitcast.17, bf16[512,128]{1,0:T(8,128)(2,1)S(1)} %bitcast.18, bf16[512,128]{1,0:T(8,128)(2,1)S(1)} %bitcast.19), custom_call_target="tpu_custom_call" | custom-call | tf_op jit(solution)/shard_map/pallas_call | solution.py:197
  15.1 0.0 copy-start
  15.1 0.8 copy-done
  15.9 131.9 %shard_map.137 = bf16[64,4096]{1,0:T(8,128)(2,1)} custom-call(bf16[512,512]{1,0:T(8,128)(2,1)} %copy-done, bf16[4096,256]{1,0:T(8,128)(2,1)} %proj_hbm.1, bf16[64,4096]{1,0:T(8,128)(2,1)} %bitcast.21, f32[1,4096]{1,0:T(1,128)} %bitcast.25, bf16[16,4096]{1,0:T(8,128)(2,1)} %bitcast.23, s32[64,2]{1,0:T(8,128)} %bitcast.24, bf16[4096,3200]{1,0:T(8,128)(2,1)} %gate_hbm.1, ...), custom_call_target="tpu_custom_call" | custom-call | tf_op jit(solution)/shard_map/pallas_call | solution.py:595
  147.8 2.4 %copy.22 = bf16[2,32,4096]{2,0,1:T(2,128)(2,1)} copy(bf16[2,32,4096]{2,1,0:T(8,128)(2,1)} %bitcast.20) | data formatting | bytes 1048576 | tf_op jit(solution)/shard_map/reshape | solution.py:650
Async XLA Ops:
  3.5 1.0 copy-start.1
  4.6 0.9 copy-start.2
  5.5 0.9 copy-start.3
  6.4 0.9 copy-start.4
  7.3 0.9 copy-start.5
  8.2 0.7 copy-start.6
  15.1 0.8 copy-start

commit v3 on v2

--- a/solution.py
+++ b/solution.py
@@ -168,16 +168,14 @@
 BF16 = jnp.bfloat16
 
 
-def attend_kernel(len_ref, q_ref, ck_ref, cv_ref, nk_ref, nv_ref, o_ref, *, seq_devs):
-    visible = len_ref[lax.axis_index("ea") // seq_devs]
+def attend(q, ck, cv, nk, nv, visible, first_row):
     contract = (((1,), (1,)), ((), ()))
-    q = q_ref[...]
-    rows, cached, fresh = q.shape[0], ck_ref.shape[0], nk_ref.shape[0]
+    rows, cached, fresh = q.shape[0], ck.shape[0], nk.shape[0]
     scale = 1.0 / math.sqrt(HD)
-    old = lax.dot_general(q, ck_ref[...], contract, preferred_element_type=F32) * scale
-    new = lax.dot_general(q, nk_ref[...], contract, preferred_element_type=F32) * scale
+    old = lax.dot_general(q, ck, contract, preferred_element_type=F32) * scale
+    new = lax.dot_general(q, nk, contract, preferred_element_type=F32) * scale
     old_pos = lax.broadcasted_iota(jnp.int32, (rows, cached), 1)
-    row_pos = lax.broadcasted_iota(jnp.int32, (rows, fresh), 0)
+    row_pos = lax.broadcasted_iota(jnp.int32, (rows, fresh), 0) + first_row
     new_pos = lax.broadcasted_iota(jnp.int32, (rows, fresh), 1)
     old = jnp.where(old_pos < visible, old, -1e30)
     new = jnp.where(new_pos <= row_pos, new, -1e30)
@@ -187,28 +185,9 @@
     old = jnp.exp(old - top)
     new = jnp.exp(new - top)
     total = jnp.sum(old, axis=1, keepdims=True) + jnp.sum(new, axis=1, keepdims=True)
-    mixed = jnp.dot(old.astype(BF16), cv_ref[...], preferred_element_type=F32)
-    mixed += jnp.dot(new.astype(BF16), nv_ref[...], preferred_element_type=F32)
-    o_ref[...] = (mixed / total).astype(BF16)
-
-
-def attend(cache_len, q, ck, cv, nk, nv):
-    rows, width = q.shape
-    return pl.pallas_call(
-        functools.partial(attend_kernel, seq_devs=KVH),
-        grid=(width // HD,),
-        out_shape=jax.ShapeDtypeStruct((rows, width), BF16),
-        in_specs=[
-            pl.BlockSpec(memory_space=pltpu.SMEM),
-            pl.BlockSpec((rows, HD), lambda h: (0, h)),
-            pl.BlockSpec(ck.shape, lambda h: (0, 0)),
-            pl.BlockSpec(cv.shape, lambda h: (0, 0)),
-            pl.BlockSpec(nk.shape, lambda h: (0, 0)),
-            pl.BlockSpec(nv.shape, lambda h: (0, 0)),
-        ],
-        out_specs=pl.BlockSpec((rows, HD), lambda h: (0, h)),
-        compiler_params=pltpu.CompilerParams(vmem_limit_bytes=40 << 20),
-    )(cache_len, q, ck, cv, nk, nv)
+    mixed = jnp.dot(old.astype(BF16), cv, preferred_element_type=F32)
+    mixed += jnp.dot(new.astype(BF16), nv, preferred_element_type=F32)
+    return (mixed / total).astype(BF16)
 
 
 def remote(src, dst, send, recv, dev):
@@ -250,12 +229,14 @@
 TILES = 5
 GU_SLOTS = 3
 DN_SLOTS = 2
+PIECES = 2
 BACK = 1024
 
 
 def layer_kernel(
-    att_ref, proj_hbm, hid_hbm, gain_ref, router_hbm, ids_ref, gate_hbm, up_hbm, down_hbm,
+    len_ref, q_hbm, ck_hbm, cv_hbm, nk_hbm, nv_hbm, proj_hbm, hid_hbm, gain_ref, router_hbm, ids_ref, gate_hbm, up_hbm, down_hbm,
     out_ref,
+    q_ref, ck_ref, cv_ref, nk_ref, nv_ref,
     buf, acc, hs, arrived, normed, proj_ref, hid_ref, router_ref, res_ref, gate_ref, place_ref,
     out_go, out_got, x, gacc, uacc, inner, back_go, back_got, fold, fold_back, terms, gu, dn,
     in_sem, gu_sem, dn_sem,
@@ -273,9 +254,12 @@
     def fetch(src, dst, slot):
         return pltpu.make_async_copy(src, dst, in_sem.at[slot])
 
-    loads = [(proj_hbm, proj_ref), (hid_hbm, hid_ref), (router_hbm, router_ref)]
-    for slot, (src, dst) in enumerate(loads):
-        fetch(src, dst, slot).start()
+    loads = [
+        (proj_hbm, proj_ref), (hid_hbm, hid_ref), (router_hbm, router_ref),
+        (q_hbm, q_ref), (ck_hbm, ck_ref), (nk_hbm, nk_ref), (cv_hbm, cv_ref), (nv_hbm, nv_ref),
+    ]
+    for slot in (3, 4, 5, 6, 7, 0, 1, 2):
+        fetch(*loads[slot], slot).start()
 
     def gate_up(u):
         h, t, slot = u // TILES, u % TILES, u % GU_SLOTS
@@ -296,39 +280,38 @@
             copy.start()
     for n in range(DN_SLOTS):
         down(n).start()
-    buf[me] = att_ref[...]
     acc[...] = jnp.zeros_like(acc)
     greet(me)
 
-    def block_copy(blk, sem, dev):
-        return remote(buf.at[blk], buf.at[blk], sem, block_sem.at[blk], dev)
-
-    def to_left(zz):
-        return block_copy(index(zz, y, c), left_sem.at[zz], index(z - 1, y, c))
-
-    def to_right(zz):
-        return block_copy(index(zz, y, c), right_sem.at[zz], index(z + 1, y, c))
-
-    def to_y(zz):
-        return block_copy(index(zz, y, c), y_sem.at[zz], index(z, 1 - y, c))
-
-    def to_core(zz, yy):
-        return block_copy(index(zz, yy, c), core_sem.at[zz * 2 + yy], index(z, y, 1 - c))
-
-    def landed(blk):
-        remote(buf.at[blk], buf.at[blk], left_sem.at[0], block_sem.at[blk], index(z, y, 1 - c)).wait_recv()
-
-    def line(zz, go_left, go_right):
+    def block_copy(p, blk, sem, dev):
+        return remote(buf.at[p, blk], buf.at[p, blk], sem, block_sem.at[p, blk], dev)
+
+    def to_left(p, zz):
+        return block_copy(p, index(zz, y, c), left_sem.at[p, zz], index(z - 1, y, c))
+
+    def to_right(p, zz):
+        return block_copy(p, index(zz, y, c), right_sem.at[p, zz], index(z + 1, y, c))
+
+    def to_y(p, zz):
+        return block_copy(p, index(zz, y, c), y_sem.at[p, zz], index(z, 1 - y, c))
+
+    def to_core(p, zz, yy):
+        return block_copy(p, index(zz, yy, c), core_sem.at[p, zz * 2 + yy], index(z, y, 1 - c))
+
+    def landed(p, blk):
+        block_copy(p, blk, left_sem.at[p, 0], index(z, y, 1 - c)).wait_recv()
+
+    def line(p, zz, go_left, go_right):
         if go_left:
             @pl.when(z > 0)
             def _():
-                to_left(zz).start()
+                to_left(p, zz).start()
         if go_right:
             @pl.when(z < NZ - 1)
             def _():
-                to_right(zz).start()
-        to_y(zz).start()
-        to_core(zz, y).start()
+                to_right(p, zz).start()
+        to_y(p, zz).start()
+        to_core(p, zz, y).start()
 
     def pair(d, step):
         @pl.when(z + d < NZ)
@@ -339,22 +322,22 @@
         def _():
             step(z - d, False)
 
-    def arrive_line(d):
+    def arrive_line(p, d):
         def step(zz, from_right):
-            landed(index(zz, y, c))
-            line(zz, from_right, not from_right)
+            landed(p, index(zz, y, c))
+            line(p, zz, from_right, not from_right)
 
         pair(d, step)
 
-    def across(zz):
-        landed(index(zz, 1 - y, c))
-        to_core(zz, 1 - y).start()
-
-    def arrive_y(d):
+    def across(p, zz):
+        landed(p, index(zz, 1 - y, c))
+        to_core(p, zz, 1 - y).start()
+
+    def arrive_y(p, d):
         if d == 0:
-            across(z)
+            across(p, z)
         else:
-            pair(d, lambda zz, _: across(zz))
+            pair(d, lambda zz, _: across(p, zz))
 
     def multiply(d):
         def go(n, carry):
@@ -370,22 +353,45 @@
 
                 @pl.when(cc == 1)
                 def _():
-                    landed(blk)
+                    for p in range(PIECES):
+                        landed(p, blk)
 
                 group = blk % KVH
-                width = buf.shape[2]
-                rows = pl.ds(pl.multiple_of(group * width, width), width)
-                acc[blk // KVH] += jnp.dot(
-                    buf[blk], proj_ref[rows, :], preferred_element_type=F32
+                total = acc[blk // KVH]
+                for p in range(PIECES):
+                    start = (group * PIECES + p) * part
+                    rows = pl.ds(pl.multiple_of(start, part), part)
+                    total += jnp.dot(
+                        buf[p, blk], proj_ref[rows, :], preferred_element_type=F32
+                    )
+                acc[blk // KVH] = total
+
+            return carry
+
+        lax.fori_loop(0, 8, go, 0)
+
+    part = buf.shape[3]
+    for slot in (3, 4, 5, 6, 7):
+        fetch(*loads[slot], slot).wait()
+    visible = len_ref[me // KVH]
+    tall = q_ref.shape[0] // 2
+    for p in range(PIECES):
+        def head(n, carry):
+            src = pl.ds(pl.multiple_of(p * part + n * HD, HD), HD)
+            dst = pl.ds(pl.multiple_of(n * HD, HD), HD)
+            for t in range(2):
+                rows = slice(t * tall, (t + 1) * tall)
+                keys = slice(0, (t + 1) * tall)
+                buf[p, me, rows, dst] = attend(
+                    q_ref[rows, src], ck_ref[...], cv_ref[...], nk_ref[keys], nv_ref[keys],
+                    visible, t * tall,
                 )
-
             return carry
 
-        lax.fori_loop(0, 8, go, 0)
-
-    line(z, True, True)
-
-    ids = ids_ref[...]
+        lax.fori_loop(0, part // HD, head, 0)
+        line(p, z, True, True)
+
+    ids = jnp.concatenate([ids_ref[:, 0, :], ids_ref[:, 1, :]], axis=0)
     lanes = lax.broadcasted_iota(jnp.int32, (ids.shape[0], EXPERTS), 1)
     count = ids.shape[0]
     first = (ids[:, 0:1] == lanes).astype(F32)
@@ -413,10 +419,12 @@
     fetch(proj_hbm, proj_ref, 0).wait()
 
     for d in range(1, NZ):
-        arrive_line(d)
-        arrive_y(d - 1)
+        for p in range(PIECES):
+            arrive_line(p, d)
+            arrive_y(p, d - 1)
         multiply(d - 1)
-    arrive_y(NZ - 1)
+    for p in range(PIECES):
+        arrive_y(p, NZ - 1)
     multiply(NZ - 1)
 
     hs[...] = acc[...].astype(BF16)
@@ -566,22 +574,23 @@
         lax.fori_loop(0, chunks, sent, 0)
 
     others(me, finish)
-    for zz in range(NZ):
-        @pl.when((z > 0) & (zz >= z))
-        def _():
-            to_left(zz).wait_send()
-
-        @pl.when((z < NZ - 1) & (zz <= z))
-        def _():
-            to_right(zz).wait_send()
-
-        to_y(zz).wait_send()
-        to_core(zz, 0).wait_send()
-        to_core(zz, 1).wait_send()
-
-
-def layer(attended, out_proj, hidden, gain, router, ids, gate_proj, up_proj, down_proj):
-    rows, width = attended.shape
+    for p in range(PIECES):
+        for zz in range(NZ):
+            @pl.when((z > 0) & (zz >= z))
+            def _():
+                to_left(p, zz).wait_send()
+
+            @pl.when((z < NZ - 1) & (zz <= z))
+            def _():
+                to_right(p, zz).wait_send()
+
+            to_y(p, zz).wait_send()
+            to_core(p, zz, 0).wait_send()
+            to_core(p, zz, 1).wait_send()
+
+
+def layer(cache_len, q, ck, cv, nk, nv, out_proj, hidden, gain, router, ids, gate_proj, up_proj, down_proj):
+    rows, width = q.shape
     seqs = NDEV // KVH
     cols = out_proj.shape[1]
     mine, model = hidden.shape
@@ -595,10 +604,18 @@
     return pl.pallas_call(
         layer_kernel,
         out_shape=jax.ShapeDtypeStruct((mine, model), BF16),
-        in_specs=[inside, outside, outside, inside, outside, inside] + [outside] * 3,
+        in_specs=[pl.BlockSpec(memory_space=pltpu.SMEM)]
+        + [outside] * 7
+        + [inside, outside, inside]
+        + [outside] * 3,
         out_specs=inside,
         scratch_shapes=[
-            pltpu.VMEM((NDEV, rows, width), BF16),
+            pltpu.VMEM(q.shape, BF16),
+            pltpu.VMEM(ck.shape, BF16),
+            pltpu.VMEM(cv.shape, BF16),
+            pltpu.VMEM(nk.shape, BF16),
+            pltpu.VMEM(nv.shape, BF16),
+            pltpu.VMEM((PIECES, NDEV, rows, width // PIECES), BF16),
             pltpu.VMEM((seqs, rows, cols), F32),
             pltpu.VMEM((seqs, rows, cols), BF16),
             pltpu.VMEM((seqs, rows // NDEV, model), BF16),
@@ -622,15 +639,15 @@
             pltpu.VMEM((SLOTS, BACK), BF16),
             pltpu.VMEM((GU_SLOTS, 2, half, TILE), BF16),
             pltpu.VMEM((DN_SLOTS, ffw, BACK), BF16),
-            dma((3,)), dma((GU_SLOTS, 2)), dma((DN_SLOTS,)),
-            dma((NDEV,)), dma((NZ,)), dma((NZ,)), dma((NZ,)), dma((2 * NZ,)),
+            dma((8,)), dma((GU_SLOTS, 2)), dma((DN_SLOTS,)), dma((PIECES, NDEV)),
+            dma((PIECES, NZ)), dma((PIECES, NZ)), dma((PIECES, NZ)), dma((PIECES, 2 * NZ)),
             dma((NDEV,)), dma((NDEV,)), dma((2, NDEV)), dma((2, NDEV)),
             dma((chunks, NDEV)), dma((chunks, NDEV)),
         ],
         compiler_params=pltpu.CompilerParams(
             collective_id=0, has_side_effects=True, vmem_limit_bytes=62 << 20
         ),
-    )(attended, out_proj, hidden, gain, router, ids, gate_proj, up_proj, down_proj)
+    )(cache_len, q, ck, cv, nk, nv, out_proj, hidden, gain, router, ids, gate_proj, up_proj, down_proj)
 
 
 def body(
@@ -638,13 +655,10 @@
     out_proj, norm_gain, router, expert_ids, gate_proj, up_proj, down_proj,
 ):
     piece, seqs, model = hidden_in.shape
-    attended = attend(
-        cache_len, queries[0], cache_keys[0], cache_values[0], new_keys[0], new_values[0]
-    )
     hidden = hidden_in.transpose(1, 0, 2).reshape(piece * seqs, model)
-    ids = expert_ids.transpose(1, 0, 2).reshape(piece * seqs, TOPK)
     out = layer(
-        attended, out_proj, hidden, norm_gain.reshape(1, model), router.T, ids,
+        cache_len, queries[0], cache_keys[0], cache_values[0], new_keys[0], new_values[0],
+        out_proj, hidden, norm_gain.reshape(1, model), router.T, expert_ids,
         gate_proj, up_proj, down_proj,
     )
     return out.reshape(seqs, piece, model).transpose(1, 0, 2)

time: 152 us -> 140 us (0.921)
  local copies, waits for them, and re-layouts: 12 us -> 5.87 us
  Pallas kernels: 138 us -> 134 us
    pallas_call x1 -> x0, Pallas kernels: 6.27 us -> none  [attend(): pl.pallas_call(functools.partial(attend_kernel, seq_devs=KVH), grid=(widt...]
    unnamed x14 -> x1, local copies, waits for them, and re-layouts: 6.1 us -> 1.37 us
    pallas_call x1, Pallas kernels: 132 us -> 134 us  [layer(): pl.pallas_call(layer_kernel, out_shape=jax.ShapeDtypeStruct((mine, model)...]
where the time goes in v3:
time: 140 us
  Pallas kernels  134 us (96%)
  local copies, waits for them, and re-layouts  5.87 us (4%)
    pallas_call x1, Pallas kernels, layer(): pl.pallas_call(layer_kernel, out_shape=jax.ShapeDtypeStruct((mine, model)...  134 us

profile of v3, /device:TPU:9, one launch (start us, length us, event | category | flops | bytes accessed | tf_op | source)
XLA Modules:
  0.0 139.6 jit_solution(1014008329739782150)
XLA Ops:
  0.0 1.4 copy.16.ids_ref
  1.4 2.1 %copy.15 = bf16[2,32,4096]{2,1,0:T(8,128)(2,1)} copy(bf16[2,32,4096]{2,0,1:T(2,128)(2,1)} %bitcast.16) | data formatting | bytes 1048576 | tf_op jit(solution)/shard_map/transpose | solution.py:658
  3.5 133.7 %shard_map.136 = bf16[64,4096]{1,0:T(8,128)(2,1)} custom-call(s32[2]{0:T(128)} %len_ref.1, bf16[512,512]{1,0:T(8,128)(2,1)} %bitcast.15, bf16[512,128]{1,0:T(8,128)(2,1)} %bitcast.17, bf16[512,128]{1,0:T(8,128)(2,1)} %bitcast.18, bf16[512,128]{1,0:T(8,128)(2,1)} %bitcast.19, bf16[512,128]{1,0:T(8,128)(2,1)} %bitcast.20, bf16[4096,256]{1,0:T(8,128)(2,1)} %proj_hbm.1, ...), custom_call_target="tpu_custom_call" | custom-call | tf_op jit(solution)/shard_map/pallas_call | solution.py:604
  137.2 2.4 %copy.19 = bf16[2,32,4096]{2,0,1:T(2,128)(2,1)} copy(bf16[2,32,4096]{2,1,0:T(8,128)(2,1)} %bitcast.13) | data formatting | bytes 1048576 | tf_op jit(solution)/shard_map/reshape | solution.py:664
